TPU v7x, 256 devices: a whole 4x4x8 slice. The times are simulated.
256 devices in a mesh: band: 16 (over z_lo, x), slab: 16 (over y, z_hi, core).
Axes of the slice: x: 4, y: 4, z: 8 (z_hi: 2, z_lo: 4; z = z_hi * 4 + z_lo), core: 2. Of those that a mesh axis runs over, the one named last changes fastest.
Arguments:
- orbitals: float32 [32, 128, 128, 128], P('band', 'slab'), may hold values from -6 to 6
- slot_ids: int32 [32], P('band'), may hold values from 0 to 31, each once
- occupations: float32 [32], replicated, may hold values from 0.25 to 2
- mode_lists: int32 [3, 48], replicated, may hold values from 0 to 127, as said below
Outputs:
- exchange_terms: float32 [32, 128, 128, 128], P('band', 'slab')
Inputs may be any that keep to these rules, and one draw needn't show every extreme that they name: `slot_ids`: each number appears once. `mode_lists`: each row lists 48 different mode numbers, among them 0 and 127.
All inputs are finite; a program needn't handle non-finite values.
Results may differ from a plain program's by a relative error of at most 0.000059.
Values sent between devices are 32-bit elements; how exact they have to be, the bound alone decides.
No kernel may reach another device: no remote copies, remote signals or barrier semaphores. Data moves between devices by JAX's collectives and lax.ppermute only.
A program may use at most 64 MiB of HBM per device.

v0:
```python
import jax
import jax.numpy as jnp
from jax import lax
from jax.sharding import PartitionSpec as P


def passed_along(value, axis, steps):
    count = lax.axis_size(axis)
    pairs = [(source, (source + steps) % count) for source in range(count)]
    return lax.ppermute(value, axis, pairs)


def sine_table(mode_row, points):
    grid = jnp.arange(points, dtype=jnp.int32) + 1
    phase = grid[:, None] * (mode_row[None, :] + 1) % (2 * points + 2)
    angle = jnp.pi * phase.astype(jnp.float32) / (points + 1.0)
    return jnp.sqrt(jnp.float32(2.0) / (points + 1.0)) * jnp.sin(angle)


def screen_table(first, second, third, points):
    squares = (
        ((first + 1) ** 2)[:, None, None]
        + ((second + 1) ** 2)[None, :, None]
        + ((third + 1) ** 2)[None, None, :]
    )
    return 1.0 / (1.0 + squares.astype(jnp.float32) / jnp.float32(points * points))


def on_device(orbitals, slot_ids, occupations, mode_lists):
    highest = lax.Precision.HIGHEST
    planes = orbitals.shape[1]
    points = orbitals.shape[2]
    count = mode_lists.shape[1]
    groups = lax.axis_size("slab")
    share = count // groups
    width = share * count
    sine_first = sine_table(mode_lists[0], points)
    sine_second = sine_table(mode_lists[1], points)
    sine_third = sine_table(mode_lists[2], points)
    local_modes = lax.dynamic_slice_in_dim(mode_lists[1], lax.axis_index("slab") * share, share)
    screen_local = screen_table(mode_lists[0], local_modes, mode_lists[2], points).reshape(
        count, width
    )
    catalog = jnp.arange(occupations.shape[0], dtype=jnp.int32)
    own_weight = jnp.sum(
        jnp.where(slot_ids[:, None] == catalog[None, :], occupations[None, :], 0.0), axis=1
    )
    own_scaled = own_weight[:, None, None, None] * orbitals

    def modal(block):
        items = block.shape[0]
        flat = block.reshape(items, points, width)
        spectral = (
            jnp.einsum("nxc,xa->nac", flat, sine_first, precision=highest) * screen_local[None]
        )
        spatial = jnp.einsum("nac,xa->nxc", spectral, sine_first, precision=highest)
        spatial = spatial.reshape(items, points, 1, width)
        return lax.all_to_all(spatial, "slab", split_axis=1, concat_axis=2, tiled=True)

    def pair_solve(left, right):
        lead = left.shape[0]
        other = right.shape[0]
        pairs = lead * other
        density = (left[:, None] * right[None, :]).reshape(pairs * planes * points, points)
        coeffs = jnp.dot(density, sine_third, precision=highest).reshape(
            pairs, planes, points, count
        )
        coeffs = jnp.einsum("nxyk,yj->nxjk", coeffs, sine_second, precision=highest)
        coeffs = coeffs.reshape(pairs, planes, groups, width)
        returned = modal(lax.all_to_all(coeffs, "slab", split_axis=2, concat_axis=1, tiled=True))
        returned = returned.reshape(pairs, planes, count, count)
        field = jnp.einsum("nxjk,yj->nxyk", returned, sine_second, precision=highest)
        field = jnp.dot(
            field.reshape(pairs * planes * points, count), sine_third.T, precision=highest
        )
        return field.reshape(lead, other, planes, points, points)

    def gathered(field, visitors, visit_weight):
        return jnp.sum(field * (visit_weight[:, None, None, None] * visitors)[None], axis=1)

    field = pair_solve(orbitals, orbitals)
    totals = jnp.sum(field * own_scaled[None], axis=1)
    bands = lax.axis_size("band")

    def visit_step(step_index, carry):
        running, visitors, visit_weight = carry
        visitors, visit_weight = passed_along((visitors, visit_weight), "band", 1)
        solved = pair_solve(orbitals, visitors)
        return (running + gathered(solved, visitors, visit_weight), visitors, visit_weight)

    result = lax.fori_loop(1, bands, visit_step, (totals, orbitals, own_weight))
    totals = result[0]
    return totals


def solution(mesh):
    in_specs = (P("band", "slab", None, None), P("band"), P(), P())
    out_specs = P("band", "slab", None, None)
    return jax.shard_map(
        on_device, mesh=mesh, in_specs=in_specs, out_specs=out_specs, check_vma=False
    )
```

profile of v0, /device:TPU:64, one launch (start us, length us, event | category | flops | bytes accessed | tf_op | source)
XLA Modules:
  0.0 1406.9 jit_solution(4840520669056700731)
XLA Ops:
  19.4 19.9 %all-to-all-done.2 = f32[4,8,16,144]{3,1,0,2:T(8,128)S(1)} async-done(((f32[4,8,16,144]{3,1,0,2:T(8,128)}), f32[4,8,16,144]{3,1,0,2:T(8,128)S(1)}, u32[]{:S(2)}, u32[]{:S(2)}) %all-to-all-start.2) | async-done | bytes 294944 | tf_op jit(solution)/shard_map/all_to_all | solution.py:70
  46.8 15.3 %all-to-all-done.3 = f32[4,128,1,144]{3,0,2,1:T(4,128)S(1)} async-done(((f32[4,128,1,144]{3,0,2,1:T(4,128)}), f32[4,128,1,144]{3,0,2,1:T(4,128)S(1)}, u32[]{:S(2)}, u32[]{:S(2)}) %all-to-all-start.3) | async-done | bytes 294944 | tf_op jit(solution)/shard_map/all_to_all | solution.py:58
  68.7 1338.2 %while.16 = (s32[]{:T(128)}, f32[2,8,128,128]{3,2,1,0:T(8,128)}, f32[2,8,128,128]{3,2,1,0:T(8,128)S(1)}, f32[2]{0:T(128)S(1)}, f32[2,8,128,128]{3,2,1,0:T(8,128)...) while((s32[]{:T(128)}, f32[2,8,128,128]{3,2,1,0:T(8,128)}, ...), condition=%wide.region_4.5_spmd.clone.clone, body=%wide.region_2.4_spmd.clone.clone.sunk | while | flops 917672704 | bytes 43984144 | solution.py:91
  70.2 25.7 %collective-permute-done = f32[2,8,128,128]{3,2,1,0:T(8,128)S(1)} collective-permute-done((f32[2,8,128,128]{3,2,1,0:T(8,128)S(1)}, f32[2,8,128,128]{3,2,1,0:T(8,128)S(1)}, u32[]{:S(2)}, u32[]{:S(2)}) %collective-permute-start) | collective-permute-done | bytes 1048608 | tf_op jit(solution)/shard_map/while/body/eval_jaxpr/ppermute | solution.py:10
  107.0 15.6 %all-to-all-done = f32[4,8,16,144]{3,1,0,2:T(8,128)S(1)} async-done(((f32[4,8,16,144]{3,1,0,2:T(8,128)}), f32[4,8,16,144]{3,1,0,2:T(8,128)S(1)}, u32[]{:S(2)}, u32[]{:S(2)}) %all-to-all-start) | async-done | bytes 294944 | tf_op jit(solution)/shard_map/while/body/eval_jaxpr/all_to_all | solution.py:70
  155.9 27.2 %collective-permute-done = f32[2,8,128,128]{3,2,1,0:T(8,128)S(1)} collective-permute-done((f32[2,8,128,128]{3,2,1,0:T(8,128)S(1)}, f32[2,8,128,128]{3,2,1,0:T(8,128)S(1)}, u32[]{:S(2)}, u32[]{:S(2)}) %collective-permute-start) | collective-permute-done | bytes 1048608 | tf_op jit(solution)/shard_map/while/body/eval_jaxpr/ppermute | solution.py:10
  194.2 15.6 %all-to-all-done = f32[4,8,16,144]{3,1,0,2:T(8,128)S(1)} async-done(((f32[4,8,16,144]{3,1,0,2:T(8,128)}), f32[4,8,16,144]{3,1,0,2:T(8,128)S(1)}, u32[]{:S(2)}, u32[]{:S(2)}) %all-to-all-start) | async-done | bytes 294944 | tf_op jit(solution)/shard_map/while/body/eval_jaxpr/all_to_all | solution.py:70
  243.1 27.2 %collective-permute-done = f32[2,8,128,128]{3,2,1,0:T(8,128)S(1)} collective-permute-done((f32[2,8,128,128]{3,2,1,0:T(8,128)S(1)}, f32[2,8,128,128]{3,2,1,0:T(8,128)S(1)}, u32[]{:S(2)}, u32[]{:S(2)}) %collective-permute-start) | collective-permute-done | bytes 1048608 | tf_op jit(solution)/shard_map/while/body/eval_jaxpr/ppermute | solution.py:10
  281.3 18.0 %all-to-all-done = f32[4,8,16,144]{3,1,0,2:T(8,128)S(1)} async-done(((f32[4,8,16,144]{3,1,0,2:T(8,128)}), f32[4,8,16,144]{3,1,0,2:T(8,128)S(1)}, u32[]{:S(2)}, u32[]{:S(2)}) %all-to-all-start) | async-done | bytes 294944 | tf_op jit(solution)/shard_map/while/body/eval_jaxpr/all_to_all | solution.py:70
  332.7 27.2 %collective-permute-done = f32[2,8,128,128]{3,2,1,0:T(8,128)S(1)} collective-permute-done((f32[2,8,128,128]{3,2,1,0:T(8,128)S(1)}, f32[2,8,128,128]{3,2,1,0:T(8,128)S(1)}, u32[]{:S(2)}, u32[]{:S(2)}) %collective-permute-start) | collective-permute-done | bytes 1048608 | tf_op jit(solution)/shard_map/while/body/eval_jaxpr/ppermute | solution.py:10
  370.9 18.0 %all-to-all-done = f32[4,8,16,144]{3,1,0,2:T(8,128)S(1)} async-done(((f32[4,8,16,144]{3,1,0,2:T(8,128)}), f32[4,8,16,144]{3,1,0,2:T(8,128)S(1)}, u32[]{:S(2)}, u32[]{:S(2)}) %all-to-all-start) | async-done | bytes 294944 | tf_op jit(solution)/shard_map/while/body/eval_jaxpr/all_to_all | solution.py:70
  422.3 27.2 %collective-permute-done = f32[2,8,128,128]{3,2,1,0:T(8,128)S(1)} collective-permute-done((f32[2,8,128,128]{3,2,1,0:T(8,128)S(1)}, f32[2,8,128,128]{3,2,1,0:T(8,128)S(1)}, u32[]{:S(2)}, u32[]{:S(2)}) %collective-permute-start) | collective-permute-done | bytes 1048608 | tf_op jit(solution)/shard_map/while/body/eval_jaxpr/ppermute | solution.py:10
  460.5 18.0 %all-to-all-done = f32[4,8,16,144]{3,1,0,2:T(8,128)S(1)} async-done(((f32[4,8,16,144]{3,1,0,2:T(8,128)}), f32[4,8,16,144]{3,1,0,2:T(8,128)S(1)}, u32[]{:S(2)}, u32[]{:S(2)}) %all-to-all-start) | async-done | bytes 294944 | tf_op jit(solution)/shard_map/while/body/eval_jaxpr/all_to_all | solution.py:70
  511.9 27.2 %collective-permute-done = f32[2,8,128,128]{3,2,1,0:T(8,128)S(1)} collective-permute-done((f32[2,8,128,128]{3,2,1,0:T(8,128)S(1)}, f32[2,8,128,128]{3,2,1,0:T(8,128)S(1)}, u32[]{:S(2)}, u32[]{:S(2)}) %collective-permute-start) | collective-permute-done | bytes 1048608 | tf_op jit(solution)/shard_map/while/body/eval_jaxpr/ppermute | solution.py:10
  550.1 18.0 %all-to-all-done = f32[4,8,16,144]{3,1,0,2:T(8,128)S(1)} async-done(((f32[4,8,16,144]{3,1,0,2:T(8,128)}), f32[4,8,16,144]{3,1,0,2:T(8,128)S(1)}, u32[]{:S(2)}, u32[]{:S(2)}) %all-to-all-start) | async-done | bytes 294944 | tf_op jit(solution)/shard_map/while/body/eval_jaxpr/all_to_all | solution.py:70
  601.4 27.2 %collective-permute-done = f32[2,8,128,128]{3,2,1,0:T(8,128)S(1)} collective-permute-done((f32[2,8,128,128]{3,2,1,0:T(8,128)S(1)}, f32[2,8,128,128]{3,2,1,0:T(8,128)S(1)}, u32[]{:S(2)}, u32[]{:S(2)}) %collective-permute-start) | collective-permute-done | bytes 1048608 | tf_op jit(solution)/shard_map/while/body/eval_jaxpr/ppermute | solution.py:10
  639.7 18.0 %all-to-all-done = f32[4,8,16,144]{3,1,0,2:T(8,128)S(1)} async-done(((f32[4,8,16,144]{3,1,0,2:T(8,128)}), f32[4,8,16,144]{3,1,0,2:T(8,128)S(1)}, u32[]{:S(2)}, u32[]{:S(2)}) %all-to-all-start) | async-done | bytes 294944 | tf_op jit(solution)/shard_map/while/body/eval_jaxpr/all_to_all | solution.py:70
  691.0 27.2 %collective-permute-done = f32[2,8,128,128]{3,2,1,0:T(8,128)S(1)} collective-permute-done((f32[2,8,128,128]{3,2,1,0:T(8,128)S(1)}, f32[2,8,128,128]{3,2,1,0:T(8,128)S(1)}, u32[]{:S(2)}, u32[]{:S(2)}) %collective-permute-start) | collective-permute-done | bytes 1048608 | tf_op jit(solution)/shard_map/while/body/eval_jaxpr/ppermute | solution.py:10
  729.2 18.0 %all-to-all-done = f32[4,8,16,144]{3,1,0,2:T(8,128)S(1)} async-done(((f32[4,8,16,144]{3,1,0,2:T(8,128)}), f32[4,8,16,144]{3,1,0,2:T(8,128)S(1)}, u32[]{:S(2)}, u32[]{:S(2)}) %all-to-all-start) | async-done | bytes 294944 | tf_op jit(solution)/shard_map/while/body/eval_jaxpr/all_to_all | solution.py:70
  780.6 27.2 %collective-permute-done = f32[2,8,128,128]{3,2,1,0:T(8,128)S(1)} collective-permute-done((f32[2,8,128,128]{3,2,1,0:T(8,128)S(1)}, f32[2,8,128,128]{3,2,1,0:T(8,128)S(1)}, u32[]{:S(2)}, u32[]{:S(2)}) %collective-permute-start) | collective-permute-done | bytes 1048608 | tf_op jit(solution)/shard_map/while/body/eval_jaxpr/ppermute | solution.py:10
  818.8 18.0 %all-to-all-done = f32[4,8,16,144]{3,1,0,2:T(8,128)S(1)} async-done(((f32[4,8,16,144]{3,1,0,2:T(8,128)}), f32[4,8,16,144]{3,1,0,2:T(8,128)S(1)}, u32[]{:S(2)}, u32[]{:S(2)}) %all-to-all-start) | async-done | bytes 294944 | tf_op jit(solution)/shard_map/while/body/eval_jaxpr/all_to_all | solution.py:70
  870.2 27.2 %collective-permute-done = f32[2,8,128,128]{3,2,1,0:T(8,128)S(1)} collective-permute-done((f32[2,8,128,128]{3,2,1,0:T(8,128)S(1)}, f32[2,8,128,128]{3,2,1,0:T(8,128)S(1)}, u32[]{:S(2)}, u32[]{:S(2)}) %collective-permute-start) | collective-permute-done | bytes 1048608 | tf_op jit(solution)/shard_map/while/body/eval_jaxpr/ppermute | solution.py:10
  908.4 18.0 %all-to-all-done = f32[4,8,16,144]{3,1,0,2:T(8,128)S(1)} async-done(((f32[4,8,16,144]{3,1,0,2:T(8,128)}), f32[4,8,16,144]{3,1,0,2:T(8,128)S(1)}, u32[]{:S(2)}, u32[]{:S(2)}) %all-to-all-start) | async-done | bytes 294944 | tf_op jit(solution)/shard_map/while/body/eval_jaxpr/all_to_all | solution.py:70
  959.8 27.2 %collective-permute-done = f32[2,8,128,128]{3,2,1,0:T(8,128)S(1)} collective-permute-done((f32[2,8,128,128]{3,2,1,0:T(8,128)S(1)}, f32[2,8,128,128]{3,2,1,0:T(8,128)S(1)}, u32[]{:S(2)}, u32[]{:S(2)}) %collective-permute-start) | collective-permute-done | bytes 1048608 | tf_op jit(solution)/shard_map/while/body/eval_jaxpr/ppermute | solution.py:10
  998.0 18.0 %all-to-all-done = f32[4,8,16,144]{3,1,0,2:T(8,128)S(1)} async-done(((f32[4,8,16,144]{3,1,0,2:T(8,128)}), f32[4,8,16,144]{3,1,0,2:T(8,128)S(1)}, u32[]{:S(2)}, u32[]{:S(2)}) %all-to-all-start) | async-done | bytes 294944 | tf_op jit(solution)/shard_map/while/body/eval_jaxpr/all_to_all | solution.py:70
  1049.4 27.2 %collective-permute-done = f32[2,8,128,128]{3,2,1,0:T(8,128)S(1)} collective-permute-done((f32[2,8,128,128]{3,2,1,0:T(8,128)S(1)}, f32[2,8,128,128]{3,2,1,0:T(8,128)S(1)}, u32[]{:S(2)}, u32[]{:S(2)}) %collective-permute-start) | collective-permute-done | bytes 1048608 | tf_op jit(solution)/shard_map/while/body/eval_jaxpr/ppermute | solution.py:10
  1087.6 18.0 %all-to-all-done = f32[4,8,16,144]{3,1,0,2:T(8,128)S(1)} async-done(((f32[4,8,16,144]{3,1,0,2:T(8,128)}), f32[4,8,16,144]{3,1,0,2:T(8,128)S(1)}, u32[]{:S(2)}, u32[]{:S(2)}) %all-to-all-start) | async-done | bytes 294944 | tf_op jit(solution)/shard_map/while/body/eval_jaxpr/all_to_all | solution.py:70
  1138.9 27.2 %collective-permute-done = f32[2,8,128,128]{3,2,1,0:T(8,128)S(1)} collective-permute-done((f32[2,8,128,128]{3,2,1,0:T(8,128)S(1)}, f32[2,8,128,128]{3,2,1,0:T(8,128)S(1)}, u32[]{:S(2)}, u32[]{:S(2)}) %collective-permute-start) | collective-permute-done | bytes 1048608 | tf_op jit(solution)/shard_map/while/body/eval_jaxpr/ppermute | solution.py:10
  1177.2 18.0 %all-to-all-done = f32[4,8,16,144]{3,1,0,2:T(8,128)S(1)} async-done(((f32[4,8,16,144]{3,1,0,2:T(8,128)}), f32[4,8,16,144]{3,1,0,2:T(8,128)S(1)}, u32[]{:S(2)}, u32[]{:S(2)}) %all-to-all-start) | async-done | bytes 294944 | tf_op jit(solution)/shard_map/while/body/eval_jaxpr/all_to_all | solution.py:70
  1228.5 32.8 %collective-permute-done = f32[2,8,128,128]{3,2,1,0:T(8,128)S(1)} collective-permute-done((f32[2,8,128,128]{3,2,1,0:T(8,128)S(1)}, f32[2,8,128,128]{3,2,1,0:T(8,128)S(1)}, u32[]{:S(2)}, u32[]{:S(2)}) %collective-permute-start) | collective-permute-done | bytes 1048608 | tf_op jit(solution)/shard_map/while/body/eval_jaxpr/ppermute | solution.py:10
  1318.1 32.0 %collective-permute-done = f32[2,8,128,128]{3,2,1,0:T(8,128)S(1)} collective-permute-done((f32[2,8,128,128]{3,2,1,0:T(8,128)S(1)}, f32[2,8,128,128]{3,2,1,0:T(8,128)S(1)}, u32[]{:S(2)}, u32[]{:S(2)}) %collective-permute-start) | collective-permute-done | bytes 1048608 | tf_op jit(solution)/shard_map/while/body/eval_jaxpr/ppermute | solution.py:10
  1361.1 14.6 %all-to-all-done = f32[4,8,16,144]{3,1,0,2:T(8,128)S(1)} async-done(((f32[4,8,16,144]{3,1,0,2:T(8,128)}), f32[4,8,16,144]{3,1,0,2:T(8,128)S(1)}, u32[]{:S(2)}, u32[]{:S(2)}) %all-to-all-start) | async-done | bytes 294944 | tf_op jit(solution)/shard_map/while/body/eval_jaxpr/all_to_all | solution.py:70
  (515 shorter events, 708.5 us)
Async XLA Ops:
  9.5 29.9 %all-to-all-start.2 = ((f32[4,8,16,144]{3,1,0,2:T(8,128)}), f32[4,8,16,144]{3,1,0,2:T(8,128)S(1)}, u32[]{:S(2)}, u32[]{:S(2)}) async-start(f32[4,8,16,144]{3,1,0,2:T(8,128)} %copy.42), calls=%async_computation.2 | async-start | bytes 1048576 | tf_op jit(solution)/shard_map/all_to_all | solution.py:70
  68.7 27.2 %collective-permute-start = (f32[2,8,128,128]{3,2,1,0:T(8,128)S(1)}, f32[2,8,128,128]{3,2,1,0:T(8,128)S(1)}, u32[]{:S(2)}, u32[]{:S(2)}) collective-permute-start(f32[2,8,128,128]{3,2,1,0:T(8,128)S(1)} %get-tuple-element.229), channel_id=1, source_target_pairs={{0,16},{16,32},{32,48},{48,64},{64,80},{80,96},{96,112},{112,128},... | collective-permute-start | bytes 3145736 | tf_op jit(solution)/shard_map/while/body/eval_jaxpr/ppermute | solution.py:10
  155.9 27.2 %collective-permute-start = (f32[2,8,128,128]{3,2,1,0:T(8,128)S(1)}, f32[2,8,128,128]{3,2,1,0:T(8,128)S(1)}, u32[]{:S(2)}, u32[]{:S(2)}) collective-permute-start(f32[2,8,128,128]{3,2,1,0:T(8,128)S(1)} %get-tuple-element.229), channel_id=1, source_target_pairs={{0,16},{16,32},{32,48},{48,64},{64,80},{80,96},{96,112},{112,128},... | collective-permute-start | bytes 3145736 | tf_op jit(solution)/shard_map/while/body/eval_jaxpr/ppermute | solution.py:10
  243.1 27.2 %collective-permute-start = (f32[2,8,128,128]{3,2,1,0:T(8,128)S(1)}, f32[2,8,128,128]{3,2,1,0:T(8,128)S(1)}, u32[]{:S(2)}, u32[]{:S(2)}) collective-permute-start(f32[2,8,128,128]{3,2,1,0:T(8,128)S(1)} %get-tuple-element.229), channel_id=1, source_target_pairs={{0,16},{16,32},{32,48},{48,64},{64,80},{80,96},{96,112},{112,128},... | collective-permute-start | bytes 3145736 | tf_op jit(solution)/shard_map/while/body/eval_jaxpr/ppermute | solution.py:10
  277.6 21.7 %all-to-all-start = ((f32[4,8,16,144]{3,1,0,2:T(8,128)}), f32[4,8,16,144]{3,1,0,2:T(8,128)S(1)}, u32[]{:S(2)}, u32[]{:S(2)}) async-start(f32[4,8,16,144]{3,1,0,2:T(8,128)} %copy.82), calls=%async_computation | async-start | bytes 1048576 | tf_op jit(solution)/shard_map/while/body/eval_jaxpr/all_to_all | solution.py:70
  332.7 27.2 %collective-permute-start = (f32[2,8,128,128]{3,2,1,0:T(8,128)S(1)}, f32[2,8,128,128]{3,2,1,0:T(8,128)S(1)}, u32[]{:S(2)}, u32[]{:S(2)}) collective-permute-start(f32[2,8,128,128]{3,2,1,0:T(8,128)S(1)} %get-tuple-element.229), channel_id=1, source_target_pairs={{0,16},{16,32},{32,48},{48,64},{64,80},{80,96},{96,112},{112,128},... | collective-permute-start | bytes 3145736 | tf_op jit(solution)/shard_map/while/body/eval_jaxpr/ppermute | solution.py:10
  367.2 21.7 %all-to-all-start = ((f32[4,8,16,144]{3,1,0,2:T(8,128)}), f32[4,8,16,144]{3,1,0,2:T(8,128)S(1)}, u32[]{:S(2)}, u32[]{:S(2)}) async-start(f32[4,8,16,144]{3,1,0,2:T(8,128)} %copy.82), calls=%async_computation | async-start | bytes 1048576 | tf_op jit(solution)/shard_map/while/body/eval_jaxpr/all_to_all | solution.py:70
  422.3 27.2 %collective-permute-start = (f32[2,8,128,128]{3,2,1,0:T(8,128)S(1)}, f32[2,8,128,128]{3,2,1,0:T(8,128)S(1)}, u32[]{:S(2)}, u32[]{:S(2)}) collective-permute-start(f32[2,8,128,128]{3,2,1,0:T(8,128)S(1)} %get-tuple-element.229), channel_id=1, source_target_pairs={{0,16},{16,32},{32,48},{48,64},{64,80},{80,96},{96,112},{112,128},... | collective-permute-start | bytes 3145736 | tf_op jit(solution)/shard_map/while/body/eval_jaxpr/ppermute | solution.py:10
  456.8 21.7 %all-to-all-start = ((f32[4,8,16,144]{3,1,0,2:T(8,128)}), f32[4,8,16,144]{3,1,0,2:T(8,128)S(1)}, u32[]{:S(2)}, u32[]{:S(2)}) async-start(f32[4,8,16,144]{3,1,0,2:T(8,128)} %copy.82), calls=%async_computation | async-start | bytes 1048576 | tf_op jit(solution)/shard_map/while/body/eval_jaxpr/all_to_all | solution.py:70
  480.8 21.2 %all-to-all-start.1 = ((f32[4,128,1,144]{3,0,2,1:T(4,128)}), f32[4,128,1,144]{3,0,2,1:T(4,128)}, u32[]{:S(2)}, u32[]{:S(2)}) async-start(f32[4,128,1,144]{3,0,2,1:T(4,128)} %copy.83), calls=%async_computation.1 | async-start | bytes 1048576 | tf_op jit(solution)/shard_map/while/body/eval_jaxpr/all_to_all | solution.py:58
  511.9 27.2 %collective-permute-start = (f32[2,8,128,128]{3,2,1,0:T(8,128)S(1)}, f32[2,8,128,128]{3,2,1,0:T(8,128)S(1)}, u32[]{:S(2)}, u32[]{:S(2)}) collective-permute-start(f32[2,8,128,128]{3,2,1,0:T(8,128)S(1)} %get-tuple-element.229), channel_id=1, source_target_pairs={{0,16},{16,32},{32,48},{48,64},{64,80},{80,96},{96,112},{112,128},... | collective-permute-start | bytes 3145736 | tf_op jit(solution)/shard_map/while/body/eval_jaxpr/ppermute | solution.py:10
  546.3 21.7 %all-to-all-start = ((f32[4,8,16,144]{3,1,0,2:T(8,128)}), f32[4,8,16,144]{3,1,0,2:T(8,128)S(1)}, u32[]{:S(2)}, u32[]{:S(2)}) async-start(f32[4,8,16,144]{3,1,0,2:T(8,128)} %copy.82), calls=%async_computation | async-start | bytes 1048576 | tf_op jit(solution)/shard_map/while/body/eval_jaxpr/all_to_all | solution.py:70
  601.4 27.2 %collective-permute-start = (f32[2,8,128,128]{3,2,1,0:T(8,128)S(1)}, f32[2,8,128,128]{3,2,1,0:T(8,128)S(1)}, u32[]{:S(2)}, u32[]{:S(2)}) collective-permute-start(f32[2,8,128,128]{3,2,1,0:T(8,128)S(1)} %get-tuple-element.229), channel_id=1, source_target_pairs={{0,16},{16,32},{32,48},{48,64},{64,80},{80,96},{96,112},{112,128},... | collective-permute-start | bytes 3145736 | tf_op jit(solution)/shard_map/while/body/eval_jaxpr/ppermute | solution.py:10
  635.9 21.7 %all-to-all-start = ((f32[4,8,16,144]{3,1,0,2:T(8,128)}), f32[4,8,16,144]{3,1,0,2:T(8,128)S(1)}, u32[]{:S(2)}, u32[]{:S(2)}) async-start(f32[4,8,16,144]{3,1,0,2:T(8,128)} %copy.82), calls=%async_computation | async-start | bytes 1048576 | tf_op jit(solution)/shard_map/while/body/eval_jaxpr/all_to_all | solution.py:70
  660.0 21.2 %all-to-all-start.1 = ((f32[4,128,1,144]{3,0,2,1:T(4,128)}), f32[4,128,1,144]{3,0,2,1:T(4,128)}, u32[]{:S(2)}, u32[]{:S(2)}) async-start(f32[4,128,1,144]{3,0,2,1:T(4,128)} %copy.83), calls=%async_computation.1 | async-start | bytes 1048576 | tf_op jit(solution)/shard_map/while/body/eval_jaxpr/all_to_all | solution.py:58
  691.0 27.2 %collective-permute-start = (f32[2,8,128,128]{3,2,1,0:T(8,128)S(1)}, f32[2,8,128,128]{3,2,1,0:T(8,128)S(1)}, u32[]{:S(2)}, u32[]{:S(2)}) collective-permute-start(f32[2,8,128,128]{3,2,1,0:T(8,128)S(1)} %get-tuple-element.229), channel_id=1, source_target_pairs={{0,16},{16,32},{32,48},{48,64},{64,80},{80,96},{96,112},{112,128},... | collective-permute-start | bytes 3145736 | tf_op jit(solution)/shard_map/while/body/eval_jaxpr/ppermute | solution.py:10
  725.5 21.7 %all-to-all-start = ((f32[4,8,16,144]{3,1,0,2:T(8,128)}), f32[4,8,16,144]{3,1,0,2:T(8,128)S(1)}, u32[]{:S(2)}, u32[]{:S(2)}) async-start(f32[4,8,16,144]{3,1,0,2:T(8,128)} %copy.82), calls=%async_computation | async-start | bytes 1048576 | tf_op jit(solution)/shard_map/while/body/eval_jaxpr/all_to_all | solution.py:70
  780.6 27.2 %collective-permute-start = (f32[2,8,128,128]{3,2,1,0:T(8,128)S(1)}, f32[2,8,128,128]{3,2,1,0:T(8,128)S(1)}, u32[]{:S(2)}, u32[]{:S(2)}) collective-permute-start(f32[2,8,128,128]{3,2,1,0:T(8,128)S(1)} %get-tuple-element.229), channel_id=1, source_target_pairs={{0,16},{16,32},{32,48},{48,64},{64,80},{80,96},{96,112},{112,128},... | collective-permute-start | bytes 3145736 | tf_op jit(solution)/shard_map/while/body/eval_jaxpr/ppermute | solution.py:10
  815.1 21.7 %all-to-all-start = ((f32[4,8,16,144]{3,1,0,2:T(8,128)}), f32[4,8,16,144]{3,1,0,2:T(8,128)S(1)}, u32[]{:S(2)}, u32[]{:S(2)}) async-start(f32[4,8,16,144]{3,1,0,2:T(8,128)} %copy.82), calls=%async_computation | async-start | bytes 1048576 | tf_op jit(solution)/shard_map/while/body/eval_jaxpr/all_to_all | solution.py:70
  839.2 21.2 %all-to-all-start.1 = ((f32[4,128,1,144]{3,0,2,1:T(4,128)}), f32[4,128,1,144]{3,0,2,1:T(4,128)}, u32[]{:S(2)}, u32[]{:S(2)}) async-start(f32[4,128,1,144]{3,0,2,1:T(4,128)} %copy.83), calls=%async_computation.1 | async-start | bytes 1048576 | tf_op jit(solution)/shard_map/while/body/eval_jaxpr/all_to_all | solution.py:58
  870.2 27.2 %collective-permute-start = (f32[2,8,128,128]{3,2,1,0:T(8,128)S(1)}, f32[2,8,128,128]{3,2,1,0:T(8,128)S(1)}, u32[]{:S(2)}, u32[]{:S(2)}) collective-permute-start(f32[2,8,128,128]{3,2,1,0:T(8,128)S(1)} %get-tuple-element.229), channel_id=1, source_target_pairs={{0,16},{16,32},{32,48},{48,64},{64,80},{80,96},{96,112},{112,128},... | collective-permute-start | bytes 3145736 | tf_op jit(solution)/shard_map/while/body/eval_jaxpr/ppermute | solution.py:10
  904.7 21.7 %all-to-all-start = ((f32[4,8,16,144]{3,1,0,2:T(8,128)}), f32[4,8,16,144]{3,1,0,2:T(8,128)S(1)}, u32[]{:S(2)}, u32[]{:S(2)}) async-start(f32[4,8,16,144]{3,1,0,2:T(8,128)} %copy.82), calls=%async_computation | async-start | bytes 1048576 | tf_op jit(solution)/shard_map/while/body/eval_jaxpr/all_to_all | solution.py:70
  959.8 27.2 %collective-permute-start = (f32[2,8,128,128]{3,2,1,0:T(8,128)S(1)}, f32[2,8,128,128]{3,2,1,0:T(8,128)S(1)}, u32[]{:S(2)}, u32[]{:S(2)}) collective-permute-start(f32[2,8,128,128]{3,2,1,0:T(8,128)S(1)} %get-tuple-element.229), channel_id=1, source_target_pairs={{0,16},{16,32},{32,48},{48,64},{64,80},{80,96},{96,112},{112,128},... | collective-permute-start | bytes 3145736 | tf_op jit(solution)/shard_map/while/body/eval_jaxpr/ppermute | solution.py:10
  994.3 21.7 %all-to-all-start = ((f32[4,8,16,144]{3,1,0,2:T(8,128)}), f32[4,8,16,144]{3,1,0,2:T(8,128)S(1)}, u32[]{:S(2)}, u32[]{:S(2)}) async-start(f32[4,8,16,144]{3,1,0,2:T(8,128)} %copy.82), calls=%async_computation | async-start | bytes 1048576 | tf_op jit(solution)/shard_map/while/body/eval_jaxpr/all_to_all | solution.py:70
  1018.3 21.2 %all-to-all-start.1 = ((f32[4,128,1,144]{3,0,2,1:T(4,128)}), f32[4,128,1,144]{3,0,2,1:T(4,128)}, u32[]{:S(2)}, u32[]{:S(2)}) async-start(f32[4,128,1,144]{3,0,2,1:T(4,128)} %copy.83), calls=%async_computation.1 | async-start | bytes 1048576 | tf_op jit(solution)/shard_map/while/body/eval_jaxpr/all_to_all | solution.py:58
  1049.3 27.2 %collective-permute-start = (f32[2,8,128,128]{3,2,1,0:T(8,128)S(1)}, f32[2,8,128,128]{3,2,1,0:T(8,128)S(1)}, u32[]{:S(2)}, u32[]{:S(2)}) collective-permute-start(f32[2,8,128,128]{3,2,1,0:T(8,128)S(1)} %get-tuple-element.229), channel_id=1, source_target_pairs={{0,16},{16,32},{32,48},{48,64},{64,80},{80,96},{96,112},{112,128},... | collective-permute-start | bytes 3145736 | tf_op jit(solution)/shard_map/while/body/eval_jaxpr/ppermute | solution.py:10
  1083.8 21.7 %all-to-all-start = ((f32[4,8,16,144]{3,1,0,2:T(8,128)}), f32[4,8,16,144]{3,1,0,2:T(8,128)S(1)}, u32[]{:S(2)}, u32[]{:S(2)}) async-start(f32[4,8,16,144]{3,1,0,2:T(8,128)} %copy.82), calls=%async_computation | async-start | bytes 1048576 | tf_op jit(solution)/shard_map/while/body/eval_jaxpr/all_to_all | solution.py:70
  1138.9 27.2 %collective-permute-start = (f32[2,8,128,128]{3,2,1,0:T(8,128)S(1)}, f32[2,8,128,128]{3,2,1,0:T(8,128)S(1)}, u32[]{:S(2)}, u32[]{:S(2)}) collective-permute-start(f32[2,8,128,128]{3,2,1,0:T(8,128)S(1)} %get-tuple-element.229), channel_id=1, source_target_pairs={{0,16},{16,32},{32,48},{48,64},{64,80},{80,96},{96,112},{112,128},... | collective-permute-start | bytes 3145736 | tf_op jit(solution)/shard_map/while/body/eval_jaxpr/ppermute | solution.py:10
  1173.4 21.7 %all-to-all-start = ((f32[4,8,16,144]{3,1,0,2:T(8,128)}), f32[4,8,16,144]{3,1,0,2:T(8,128)S(1)}, u32[]{:S(2)}, u32[]{:S(2)}) async-start(f32[4,8,16,144]{3,1,0,2:T(8,128)} %copy.82), calls=%async_computation | async-start | bytes 1048576 | tf_op jit(solution)/shard_map/while/body/eval_jaxpr/all_to_all | solution.py:70
  1197.5 21.2 %all-to-all-start.1 = ((f32[4,128,1,144]{3,0,2,1:T(4,128)}), f32[4,128,1,144]{3,0,2,1:T(4,128)}, u32[]{:S(2)}, u32[]{:S(2)}) async-start(f32[4,128,1,144]{3,0,2,1:T(4,128)} %copy.83), calls=%async_computation.1 | async-start | bytes 1048576 | tf_op jit(solution)/shard_map/while/body/eval_jaxpr/all_to_all | solution.py:58
  1228.5 32.9 %collective-permute-start = (f32[2,8,128,128]{3,2,1,0:T(8,128)S(1)}, f32[2,8,128,128]{3,2,1,0:T(8,128)S(1)}, u32[]{:S(2)}, u32[]{:S(2)}) collective-permute-start(f32[2,8,128,128]{3,2,1,0:T(8,128)S(1)} %get-tuple-element.229), channel_id=1, source_target_pairs={{0,16},{16,32},{32,48},{48,64},{64,80},{80,96},{96,112},{112,128},... | collective-permute-start | bytes 3145736 | tf_op jit(solution)/shard_map/while/body/eval_jaxpr/ppermute | solution.py:10
  1318.1 32.0 %collective-permute-start = (f32[2,8,128,128]{3,2,1,0:T(8,128)S(1)}, f32[2,8,128,128]{3,2,1,0:T(8,128)S(1)}, u32[]{:S(2)}, u32[]{:S(2)}) collective-permute-start(f32[2,8,128,128]{3,2,1,0:T(8,128)S(1)} %get-tuple-element.229), channel_id=1, source_target_pairs={{0,16},{16,32},{32,48},{48,64},{64,80},{80,96},{96,112},{112,128},... | collective-permute-start | bytes 3145736 | tf_op jit(solution)/shard_map/while/body/eval_jaxpr/ppermute | solution.py:10
  (79 other events, 550.1 us)
where the time goes:
time: 1410 us
  waiting for transfers between devices  941 us (67%)
  matrix products  172 us (12%)
  local copies, waits for them, and re-layouts  143 us (10%)
  starting transfers between devices  134 us (10%)
    ppermute x30, waiting for transfers between devices, passed_along(): return lax.ppermute(value, axis, pairs)  501 us
    all_to_all x16, waiting for transfers between devices, pair_solve(): lax.all_to_all(coeffs, 'slab', split_axis=2, concat_axis=1, tiled=True)  278 us
    all_to_all x16, waiting for transfers between devices, modal(): lax.all_to_all(spatial, 'slab', split_axis=1, concat_axis=2, tiled=True)  161 us
    all_to_all x16, starting transfers between devices, modal(): lax.all_to_all(spatial, 'slab', split_axis=1, concat_axis=2, tiled=True)  67.5 us
    all_to_all x16, starting transfers between devices, pair_solve(): lax.all_to_all(coeffs, 'slab', split_axis=2, concat_axis=1, tiled=True)  63.1 us
    dot_general x16, matrix products, pair_solve(): jnp.dot(field.reshape(pairs * planes * points, count), sine_third.T, prec...  57.2 us
    dot_general x16, matrix products, pair_solve(): jnp.dot(density, sine_third, precision=highest)  40.5 us
    all_to_all x32, local copies, waits for them, and re-layouts, modal(): lax.all_to_all(spatial, 'slab', split_axis=1, concat_axis=2, tiled=True)  32.5 us
  transfers between devices with their start and end apart: 62, of which 62 were waited for; matrix products, arithmetic and copies ran while one was open for 1% of the time, Pallas kernels for 0%

commit v1 on v0

v1 whole, which is shorter than its diff:
```python
import functools

import jax
import jax.numpy as jnp
from jax import lax
from jax.experimental import pallas as pl
from jax.experimental.pallas import tpu as pltpu
from jax.sharding import Mesh
from jax.sharding import PartitionSpec as P


MODES = ("y", "core")
BLOCK = 2


def sine_table(left, right, points):
    phase = (left[:, None] + 1) * (right[None, :] + 1) % (2 * points + 2)
    angle = jnp.pi * phase.astype(jnp.float32) / (points + 1.0)
    return jnp.sqrt(jnp.float32(2.0) / (points + 1.0)) * jnp.sin(angle)


def screen_table(first, second, third, points):
    squares = (
        ((first + 1) ** 2)[:, None, None]
        + ((second + 1) ** 2)[None, :, None]
        + ((third + 1) ** 2)[None, None, :]
    )
    return 1.0 / (1.0 + squares.astype(jnp.float32) / jnp.float32(points * points))


def halves(value):
    high = value.astype(jnp.bfloat16)
    low = (value - high.astype(jnp.float32)).astype(jnp.bfloat16)
    return high, low


def table_halves(value):
    high = lax.reduce_precision(value, exponent_bits=8, mantissa_bits=7)
    return high.astype(jnp.bfloat16), (value - high).astype(jnp.bfloat16)


def dot3(left, right):
    mul = functools.partial(jnp.dot, preferred_element_type=jnp.float32)
    return mul(left[0], right[0]) + (mul(left[1], right[0]) + mul(left[0], right[1]))


def window(step, count, pairs=2):
    first = 2 * step * count // 128 * 128
    last = (2 * step + pairs) * count
    return first, -(-(last - first) // 128) * 128


def lanes_of(pairs, count):
    return -(-len(pairs) * count // 128) * 128


def loaded(refs, flags, spot):
    if len(spot) == 2:
        return refs[spot[0]][spot[1]]
    flag, (a, i), (b, j) = spot
    return jnp.where(flags[flag] != 0, refs[a][i], refs[b][j])


def added(refs, flags, spot, term):
    if len(spot) == 2:
        refs[spot[0]][spot[1]] += term
    else:
        flag, (a, i), (b, j) = spot
        chosen = flags[flag] != 0
        refs[a][i] += jnp.where(chosen, term, 0.0)
        refs[b][j] += jnp.where(chosen, 0.0, term)


def forward_kernel(pairs, count, n_arrays, flags, *refs):
    arrays = refs[:n_arrays]
    wide_hi, wide_lo, flip_hi, flip_lo, out = refs[n_arrays:]
    points = wide_hi.shape[1] // 2
    tall = out.shape[0] // count
    tiles = [None] * (tall // 8)
    for step in range(-(-len(pairs) // 2)):
        couple = pairs[2 * step : 2 * step + 2]
        parts = [
            (loaded(arrays, flags, f) * loaded(arrays, flags, s)).reshape(-1, points)
            for f, s in couple
        ]
        density = parts[0] if len(parts) == 1 else jnp.concatenate(parts, axis=1)
        deep = density.shape[1]
        first, width = window(step, count, len(parts))
        made = dot3(
            halves(density), (wide_hi[step % 4, :deep, :width], wide_lo[step % 4, :deep, :width])
        )
        for part in range(width // 128):
            tile = first // 128 + part
            piece = made[:, part * 128 : part * 128 + 128]
            tiles[tile] = piece if tiles[tile] is None else tiles[tile] + piece
    whole = jnp.concatenate(tiles, axis=1)
    flip = (flip_hi[...], flip_lo[...])
    for plane in range(BLOCK):
        made = dot3(flip, halves(whole[plane * points : (plane + 1) * points]))
        for tile in range(len(tiles)):
            start = tile * 8 + pl.program_id(0) * BLOCK + plane
            out[pl.ds(start, count, stride=tall), :] = made[:, tile * 128 : tile * 128 + 128]


def inverse_kernel(pairs, count, n_arrays, had, flags, *refs):
    arrays = refs[:n_arrays]
    before = refs[n_arrays : n_arrays + sum(had)]
    given, tall_hi, tall_lo, back_hi, back_lo = refs[n_arrays + sum(had) :][:5]
    outs = refs[n_arrays + sum(had) + 5 :]
    points = back_hi.shape[0]
    tall = given.shape[0] // count
    taken = iter(before)
    for out, old in zip(outs, had):
        out[...] = next(taken)[...] if old else jnp.zeros_like(out)
    back = (back_hi[...], back_lo[...])
    planes = []
    for plane in range(BLOCK):
        start = pl.program_id(0) * BLOCK + plane
        got = [given[pl.ds(tile + start, count, stride=tall), :] for tile in range(0, tall, 8)]
        planes.append(dot3(back, halves(jnp.concatenate(got, axis=1))))
    high, low = halves(jnp.concatenate(planes, axis=0))
    for step in range(-(-len(pairs) // 2)):
        couple = pairs[2 * step : 2 * step + 2]
        first, width = window(step, count, len(couple))
        wide = 128 * len(couple)
        field = dot3(
            (high[:, first : first + width], low[:, first : first + width]),
            (tall_hi[step % 4, :width, :wide], tall_lo[step % 4, :width, :wide]),
        )
        for place, (f, s) in enumerate(couple):
            piece = field[:, place * 128 : place * 128 + 128].reshape(BLOCK, points, points)
            added(outs, flags, f, loaded(arrays, flags, s) * piece)
            if f != s:
                added(outs, flags, s, loaded(arrays, flags, f) * piece)


def slab_spec(array):
    return pl.BlockSpec((array.shape[0], BLOCK) + array.shape[2:], lambda x: (0, x, 0, 0))


def whole_spec(array):
    return pl.BlockSpec(array.shape, lambda x: (0,) * array.ndim)


SCALARS = pl.BlockSpec(memory_space=pltpu.SMEM)


def forward(arrays, pairs, tables):
    count = tables["flip"][0].shape[0]
    planes, points = arrays[0].shape[1:3]
    lanes = lanes_of(pairs, count)
    fixed = [*tables["wide"], *tables["flip"]]
    flops = len(pairs) * planes * points * (points + count) * count * 6
    return pl.pallas_call(
        functools.partial(forward_kernel, pairs, count, len(arrays)),
        grid=(planes // BLOCK,),
        in_specs=[SCALARS] + [slab_spec(a) for a in arrays] + [whole_spec(a) for a in fixed],
        out_specs=pl.BlockSpec((count * planes * lanes // 128, 128), lambda x: (0, 0)),
        out_shape=jax.ShapeDtypeStruct((count * planes * lanes // 128, 128), jnp.float32),
        cost_estimate=pl.CostEstimate(flops=8 * flops, transcendentals=0, bytes_accessed=8 << 20),
        name="pairs_forward",
    )(tables["flags"], *arrays, *fixed)


def inverse(given, arrays, pairs, before, tables):
    count = tables["flip"][0].shape[0]
    planes, points = arrays[0].shape[1:3]
    fixed = [given, *tables["tall"], *tables["back"]]
    had = tuple(b is not None for b in before)
    olds = [b for b in before if b is not None]
    flops = len(pairs) * planes * points * (points + count) * count * 6
    return pl.pallas_call(
        functools.partial(inverse_kernel, pairs, count, len(arrays), had),
        grid=(planes // BLOCK,),
        in_specs=[SCALARS]
        + [slab_spec(a) for a in [*arrays, *olds]]
        + [whole_spec(a) for a in fixed],
        out_specs=[slab_spec(a) for a in arrays],
        out_shape=[jax.ShapeDtypeStruct(a.shape, jnp.float32) for a in arrays],
        cost_estimate=pl.CostEstimate(flops=8 * flops, transcendentals=0, bytes_accessed=12 << 20),
        name="pairs_inverse",
    )(tables["flags"], *arrays, *olds, *fixed)


def spectral_kernel(given, turned_hi, turned_lo, out):
    groups, share, tiles, planes, wide = given.shape
    turned = (turned_hi[...], turned_lo[...])
    for mode in range(share):
        blocks = [given[:, mode, t].reshape(groups * planes, wide) for t in range(tiles)]
        made = dot3(turned, halves(jnp.concatenate(blocks, axis=1)))
        for t in range(tiles):
            out[mode, t] = made[:, t * wide : (t + 1) * wide]


def spatial_kernel(here, other, screen, first_hi, first_lo, out):
    groups, share, tiles, planes, wide = out.shape
    first = (first_hi[...], first_lo[...])
    for mode in range(share):
        parts = [(here[mode, t] + other[mode, t]) * screen[mode, t] for t in range(tiles)]
        made = dot3(first, halves(jnp.concatenate(parts, axis=1)))
        for t in range(tiles):
            out[:, mode, t] = made[:, t * wide : (t + 1) * wide].reshape(groups, planes, wide)


def to_spectral(given, tables):
    share, tiles = given.shape[1:3]
    count, rows = tables["turned"][0].shape
    return pl.pallas_call(
        spectral_kernel,
        out_shape=jax.ShapeDtypeStruct((share, tiles, count, 128), jnp.float32),
        cost_estimate=pl.CostEstimate(
            flops=40 * rows * count * share * tiles * 128,
            transcendentals=0,
            bytes_accessed=8 * given.size,
        ),
        name="to_spectral",
    )(given, *tables["turned"])


def to_spatial(here, other, shape, tables):
    share, tiles, count, _ = here.shape
    rows = tables["first"][0].shape[0]
    return pl.pallas_call(
        spatial_kernel,
        out_shape=jax.ShapeDtypeStruct(shape, jnp.float32),
        cost_estimate=pl.CostEstimate(
            flops=40 * rows * count * share * tiles * 128,
            transcendentals=0,
            bytes_accessed=12 * here.size,
        ),
        name="to_spatial",
    )(here, other, tables["screen"], *tables["first"])


def make_tables(mode_lists, points):
    count = mode_lists.shape[1]
    share = count // lax.axis_size(MODES)
    grid = jnp.arange(points, dtype=jnp.int32)
    third = sine_table(grid, mode_lists[2], points)
    third_turned = sine_table(mode_lists[2], grid, points)
    here = grid.reshape(lax.axis_size("y"), lax.axis_size("z_hi"), -1)
    here = lax.dynamic_index_in_dim(here, lax.axis_index("z_hi"), 1, keepdims=False).reshape(-1)
    local = lax.dynamic_slice_in_dim(mode_lists[1], lax.axis_index(MODES) * share, share)
    screen = screen_table(local, mode_lists[0], mode_lists[2], points)
    screen = jnp.tile(screen, (1, 1, 16)).reshape(share, count, -1, 128).transpose(0, 2, 1, 3)
    wide = []
    tall = []
    for step in range(4):
        offset = 2 * step * count - window(step, count)[0]
        rest = 256 - offset - count
        wide.append(
            jnp.pad(third, ((0, points), (offset, rest)))
            + jnp.pad(third, ((points, 0), (offset + count, rest - count)))
        )
        tall.append(
            jnp.pad(third_turned, ((offset, rest), (0, points)))
            + jnp.pad(third_turned, ((offset + count, rest - count), (points, 0)))
        )
    return {
        "wide": table_halves(jnp.stack(wide)),
        "tall": table_halves(jnp.stack(tall)),
        "flip": table_halves(sine_table(mode_lists[1], grid, points)),
        "back": table_halves(sine_table(grid, mode_lists[1], points)),
        "first": table_halves(sine_table(here, mode_lists[0], points)),
        "turned": table_halves(sine_table(mode_lists[0], here, points)),
        "screen": screen,
    }


def moved(value, axis, steps):
    size = lax.axis_size(axis)
    pairs = [((place + steps) % size, place) for place in range(size)]
    return lax.ppermute(value, axis, pairs)


def on_device(orbitals, slot_ids, occupations, mode_lists):
    planes, points = orbitals.shape[1:3]
    groups = lax.axis_size(MODES)
    count = mode_lists.shape[1]
    share = count // groups
    catalog = jnp.arange(occupations.shape[0], dtype=jnp.int32)
    weight = jnp.sum(
        jnp.where(slot_ids[:, None] == catalog[None, :], occupations[None, :], 0.0), axis=1
    )
    root = jnp.sqrt(weight)[:, None, None, None]
    o = orbitals * root
    v = moved(o, "z_lo", 1)
    a = moved(o, "x", 1)
    c = moved(o, "x", -1)
    w = moved(v, "z_lo", 1)
    tables = make_tables(mode_lists, points)
    sides = [lax.axis_index(n) < lax.axis_size(n) // 2 for n in ("x", "z_lo")]
    tables["flags"] = jnp.stack(sides).astype(jnp.int32)
    tables, a = lax.optimization_barrier((tables, a))
    b = moved(a, "x", 1)
    arrays = {"o": o, "a": a, "b": b, "c": c, "v": v, "w": w}
    chosen = {
        "p0": (0, "o0", "b1"),
        "p1": (0, "b0", "o0"),
        "p2": (0, "b1", "o1"),
        "d0": (1, "o0", "b0"),
        "d1": (1, "o1", "b1"),
    }

    def product(first, second):
        return [(first + i, second + j) for i in "01" for j in "01"]

    chunks = [
        product("v", "a") + product("v", "c") + product("o", "a") + [("o0", "o1")],
        product("w", "a") + product("w", "d") + [("o0", "o0"), ("o1", "o1")],
        product("v", "o") + product("v", "b") + [("p0", "p1"), ("p0", "p2")],
    ]

    def parts(name):
        return chosen[name][1:] if name in chosen else (name,)

    names = [
        sorted({part[0] for pair in chunk for name in pair for part in parts(name)})
        for chunk in chunks
    ]

    def spot(k, name):
        if name in chosen:
            flag, first, second = chosen[name]
            return (flag, spot(k, first), spot(k, second))
        return (names[k].index(name[0]), int(name[1]))

    indexed = [[tuple(spot(k, n) for n in pair) for pair in chunk] for k, chunk in enumerate(chunks)]

    def exchange(value):
        return lax.all_to_all(value, MODES, split_axis=0, concat_axis=0, tiled=True)

    def pairs_there(k):
        made = forward([arrays[n] for n in names[k]], indexed[k], tables)
        return exchange(made.reshape(groups, share, -1, planes, 128))

    def swapped(got):
        here = to_spectral(got, tables)
        return here, moved(here, "z_hi", 1)

    sums = {}

    def collect(k, here, other, shape):
        field = to_spatial(here, other, shape, tables)
        field = exchange(field).reshape(-1, 128)
        before = [sums.get(n) for n in names[k]]
        taken = [arrays[n] for n in names[k]]
        made = inverse(field, taken, indexed[k], before, tables)
        sums.update(zip(names[k], made))

    got = [pairs_there(k) for k in range(3)]
    here0, other0 = swapped(got[0])
    here1, other1 = swapped(got[1])
    here2 = to_spectral(got[2], tables)
    here2, other1 = lax.optimization_barrier((here2, other1))
    other2 = moved(here2, "z_hi", 1)
    collect(0, here0, other0, got[0].shape)
    collect(1, here1, other1, got[1].shape)
    sums["w"], other2 = lax.optimization_barrier((sums["w"], other2))
    home = [moved(sums["a"], "x", -1), moved(sums["c"], "x", 1)]
    to_v = moved(sums["w"], "z_lo", -1)
    collect(2, here2, other2, got[2].shape)
    home += [moved(sums["b"], "x", -2), moved(sums["v"] + to_v, "z_lo", -1)]
    total = sums["o"]
    for part in home:
        total = total + part
    return total / root


def solution(mesh):
    names = ("z_lo", "x", "y", "z_hi", "core")
    fine = Mesh(mesh.devices.reshape(4, 4, 4, 2, 2), names)
    placed = P(names[:2], names[2:], None, None)
    in_specs = (placed, P(names[:2]), P(), P())

    return jax.shard_map(on_device, mesh=fine, in_specs=in_specs, out_specs=placed, check_vma=False)
```

time: 1410 us -> 259 us (0.18)
  waiting for transfers between devices: 941 us -> 117 us
  matrix products: 172 us -> 0 us
  local copies, waits for them, and re-layouts: 143 us -> 6.81 us
  starting transfers between devices: 134 us -> 53.6 us
  Pallas kernels: 0 us -> 60.3 us
    all_to_all x32 -> x6, waiting for transfers between devices: 439 us -> 10.3 us  [exchange(): return lax.all_to_all(value, MODES, split_axis=0, concat_axis=0, tiled=True)]
    ppermute x30 -> x13, waiting for transfers between devices: 501 us -> 107 us  [moved(): return lax.ppermute(value, axis, pairs)]
    dot_general x96 -> x0, matrix products: 172 us -> none  [the longest x16 57.2 us: pair_solve(): jnp.dot(field.reshape(pairs * planes * points, count), sine_third.T, prec...]
    all_to_all x32 -> x6, starting transfers between devices: 131 us -> 27 us  [exchange(): return lax.all_to_all(value, MODES, split_axis=0, concat_axis=0, tiled=True)]
    pallas_call x0 -> x12, Pallas kernels: none -> 60.3 us  [the longest x3 24 us: inverse(): pl.pallas_call(functools.partial(inverse_kernel, pairs, count, len(arrays...]
    reshape x64 -> x0, local copies, waits for them, and re-layouts: 58.7 us -> none  [the longest x16 21.7 us: pair_solve(): returned = returned.reshape(pairs, planes, count, count)]
    all_to_all x32 -> x0, local copies, waits for them, and re-layouts: 32.5 us -> none  [modal(): lax.all_to_all(spatial, 'slab', split_axis=1, concat_axis=2, tiled=True)]
    while x120 -> x0, local copies, waits for them, and re-layouts: 29.3 us -> none
  transfers between devices with their start and end apart: 62 -> 19, of which waited for: 62 -> 10; matrix products, arithmetic and copies ran while one was open for 1% -> 5% of each run, Pallas kernels for 0% -> 23%
where the time goes in v1:
time: 259 us; the launch traced here: 254 us
  waiting for transfers between devices  117 us (45%)
  Pallas kernels  60.3 us (23%)
  starting transfers between devices  53.6 us (21%)
  other arithmetic  15.7 us (6%)
  local copies, waits for them, and re-layouts  6.81 us (3%)
    ppermute x13, waiting for transfers between devices, moved(): return lax.ppermute(value, axis, pairs)  107 us
    all_to_all x6, starting transfers between devices, exchange(): return lax.all_to_all(value, MODES, split_axis=0, concat_axis=0, tiled=True)  27 us
    ppermute x13, starting transfers between devices, moved(): return lax.ppermute(value, axis, pairs)  26.6 us
    pallas_call x3, Pallas kernels, inverse(): pl.pallas_call(functools.partial(inverse_kernel, pairs, count, len(arrays...  24 us
    pallas_call x3, Pallas kernels, forward(): pl.pallas_call(functools.partial(forward_kernel, pairs, count, len(arrays...  20 us
    all_to_all x6, waiting for transfers between devices, exchange(): return lax.all_to_all(value, MODES, split_axis=0, concat_axis=0, tiled=True)  10.3 us
    pallas_call x3, Pallas kernels, to_spatial(): pl.pallas_call(spatial_kernel, out_shape=jax.ShapeDtypeStruct(shape, jnp....  8.93 us
    pallas_call x3, Pallas kernels, to_spectral(): pl.pallas_call(spectral_kernel, out_shape=jax.ShapeDtypeStruct((share, ti...  7.37 us
  transfers between devices with their start and end apart: 19, of which 10 were waited for; matrix products, arithmetic and copies ran while one was open for 5% of the time, Pallas kernels for 23%

profile of v1, /device:TPU:64, one launch (start us, length us, event | category | flops | bytes accessed | tf_op | source)
XLA Modules:
  0.0 253.9 jit_solution(13303012866363165790)
XLA Ops:
  0.9 2.4 broadcast_multiply_fusion.refs_2_.refs_1_
  3.2 2.8 %collective-permute-start = (f32[2,8,128,128]{3,2,1,0:T(8,128)}, f32[2,8,128,128]{3,2,1,0:T(8,128)}, u32[]{:S(2)}, u32[]{:S(2)}) collective-permute-start(f32[2,8,128,128]{3,2,1,0:T(8,128)} %broadcast_multiply_fusion.refs_2_.refs_1_), channel_id=1, source_target_pairs={{16,0},{32,16},{48,32},{0,48},{17,1},{33,17},{49,33},{1,49},{18,2}... | collective-permute-start | bytes 3145736 | tf_op jit(solution)/shard_map/ppermute | solution.py:273
  18.3 10.4 %collective-permute-done.refs_0_ = f32[2,8,128,128]{3,2,1,0:T(8,128)} collective-permute-done((f32[2,8,128,128]{3,2,1,0:T(8,128)}, f32[2,8,128,128]{3,2,1,0:T(8,128)}, u32[]{:S(2)}, u32[]{:S(2)}) %collective-permute-start) | collective-permute-done | bytes 1048608 | tf_op jit(solution)/shard_map/ppermute | solution.py:273
  28.7 3.7 %collective-permute-start.1 = (f32[2,8,128,128]{3,2,1,0:T(8,128)}, f32[2,8,128,128]{3,2,1,0:T(8,128)S(1)}, u32[]{:S(2)}, u32[]{:S(2)}) collective-permute-start(f32[2,8,128,128]{3,2,1,0:T(8,128)} %collective-permute-done.refs_0_), channel_id=1, source_target_pairs={{16,0},{32,16},{48,32},{0,48},{17,1},{33,17},{49,33},{1,49},{18,2}... | collective-permute-start | bytes 3145736 | tf_op jit(solution)/shard_map/ppermute | solution.py:273
  32.4 7.0 %pairs_forward.3 = f32[1920,128]{1,0:T(8,128)} custom-call(s32[2]{0:T(128)} %add_convert_fusion.flags, f32[2,8,128,128]{3,2,1,0:T(8,128)} %collective-permute-done.refs_0_, f32[2,8,128,128]{3,2,1,0:T(8,128)} %collective-permute-done.4.refs_1_, f32[2,8,128,128]{3,2,1,0:T(8,128)} %broadcast_multiply_fusion.refs_2_.refs_1_, ...), custom_call_target="tpu_custom_call" | custom-call | flops 5398069248 | bytes 8388608 | tf_op jit(solution)/shard_map/pairs_forward/pallas_call | solution.py:154
  39.5 4.5 %all-to-all-start = ((f32[8,6,5,8,128]{4,3,2,1,0:T(8,128)}), f32[8,6,5,8,128]{4,3,2,1,0:T(8,128)S(1)}, u32[]{:S(2)}, u32[]{:S(2)}) async-start(f32[8,6,5,8,128]{4,3,2,1,0:T(8,128)} %bitcast.47), calls=%async_computation | async-start | bytes 1966080 | tf_op jit(solution)/shard_map/all_to_all | solution.py:331
  44.0 10.3 %collective-permute-done.1.refs_1_.refs_0_ = f32[2,8,128,128]{3,2,1,0:T(8,128)S(1)} collective-permute-done((f32[2,8,128,128]{3,2,1,0:T(8,128)}, f32[2,8,128,128]{3,2,1,0:T(8,128)S(1)}, u32[]{:S(2)}, u32[]{:S(2)}) %collective-permute-start.1) | collective-permute-done | bytes 1048608 | tf_op jit(solution)/shard_map/ppermute | solution.py:273
  55.3 6.4 %pairs_forward.5 = f32[1536,128]{1,0:T(8,128)} custom-call(s32[2]{0:T(128)} %add_convert_fusion.flags, f32[2,8,128,128]{3,2,1,0:T(8,128)} %copy-done.15, f32[2,8,128,128]{3,2,1,0:T(8,128)} %broadcast_multiply_fusion.refs_2_.refs_1_, f32[2,8,128,128]{3,2,1,0:T(8,128)} %collective-permute-done.2.refs_3_.refs_2_, ...), custom_call_target="tpu_custom_call" | custom-call | flops 4152360960 | bytes 8388608 | tf_op jit(solution)/shard_map/pairs_forward/pallas_call | solution.py:154
  61.6 4.5 %all-to-all-start.3 = ((f32[8,6,4,8,128]{4,3,2,1,0:T(8,128)}), f32[8,6,4,8,128]{4,3,2,1,0:T(8,128)S(1)}, u32[]{:S(2)}, u32[]{:S(2)}) async-start(f32[8,6,4,8,128]{4,3,2,1,0:T(8,128)} %bitcast.49), calls=%async_computation.3 | async-start | bytes 1572864 | tf_op jit(solution)/shard_map/all_to_all | solution.py:331
  66.1 2.7 %to_spectral.3.here = f32[6,5,48,128]{3,2,1,0:T(8,128)} custom-call(f32[8,6,5,8,128]{4,3,2,1,0:T(8,128)} %copy-done.9, bf16[48,64]{1,0:T(8,128)(2,1)} %get-tuple-element.41.turned_hi, bf16[48,64]{1,0:T(8,128)(2,1)} %get-tuple-element.42.turned_lo), custom_call_target="tpu_custom_call" | custom-call | flops 471859200 | bytes 1966080 | tf_op jit(solution)/shard_map/to_spectral/pallas_call | solution.py:208
  68.8 5.4 %collective-permute-start.5 = (f32[6,5,48,128]{3,2,1,0:T(8,128)}, f32[6,5,48,128]{3,2,1,0:T(8,128)S(1)}, u32[]{:S(2)}, u32[]{:S(2)}) collective-permute-start(f32[6,5,48,128]{3,2,1,0:T(8,128)} %to_spectral.3.here), channel_id=1, source_target_pairs={{2,0},{0,2},{3,1},{1,3},{6,4},{4,6},{7,5},{5,7},{10,8},{8,10},{11,... | collective-permute-start | bytes 2211848 | tf_op jit(solution)/shard_map/ppermute | solution.py:273
  74.2 6.7 %pairs_forward.4 = f32[1536,128]{1,0:T(8,128)} custom-call(s32[2]{0:T(128)} %add_convert_fusion.flags, f32[2,8,128,128]{3,2,1,0:T(8,128)} %collective-permute-done.refs_0_, f32[2,8,128,128]{3,2,1,0:T(8,128)} %copy-done.15, f32[2,8,128,128]{3,2,1,0:T(8,128)} %broadcast_multiply_fusion.refs_2_.refs_1_, f32[2,8,128,128]{3,2,1,0:T(8,128)} %collective-permute-done.3.refs_3_, ...), custom_call_target="tpu_custom_call" | custom-call | flops 4152360960 | bytes 8388608 | tf_op jit(solution)/shard_map/pairs_forward/pallas_call | solution.py:154
  80.9 4.8 %all-to-all-start.2 = ((f32[8,6,4,8,128]{4,3,2,1,0:T(8,128)}), f32[8,6,4,8,128]{4,3,2,1,0:T(8,128)S(1)}, u32[]{:S(2)}, u32[]{:S(2)}) async-start(f32[8,6,4,8,128]{4,3,2,1,0:T(8,128)} %bitcast.50), calls=%async_computation.2 | async-start | bytes 1572864 | tf_op jit(solution)/shard_map/all_to_all | solution.py:331
  85.7 22.4 %collective-permute-done.5.other = f32[6,5,48,128]{3,2,1,0:T(8,128)S(1)} collective-permute-done((f32[6,5,48,128]{3,2,1,0:T(8,128)}, f32[6,5,48,128]{3,2,1,0:T(8,128)S(1)}, u32[]{:S(2)}, u32[]{:S(2)}) %collective-permute-start.5) | collective-permute-done | bytes 737312 | tf_op jit(solution)/shard_map/ppermute | solution.py:273
  108.9 3.1 %to_spatial.3 = f32[8,6,5,8,128]{4,3,2,1,0:T(8,128)} custom-call(f32[6,5,48,128]{3,2,1,0:T(8,128)} %to_spectral.3.here, f32[6,5,48,128]{3,2,1,0:T(8,128)} %copy-done.11, f32[6,6,48,128]{3,2,1,0:T(8,128)} %bitcast.43, bf16[64,48]{1,0:T(8,128)(2,1)} %get-tuple-element.44.first_hi, bf16[64,48]{1,0:T(8,128)(2,1)} %get-tuple-element.45.first_lo), custom_call_target="tpu_custom_call" | custom-call | flops 471859200 | bytes 2211840 | tf_op jit(solution)/shard_map/to_spatial/pallas_call | solution.py:223
  112.1 4.4 %all-to-all-start.1 = ((f32[8,6,5,8,128]{4,3,2,1,0:T(8,128)}), f32[8,6,5,8,128]{4,3,2,1,0:T(8,128)S(1)}, u32[]{:S(2)}, u32[]{:S(2)}) async-start(f32[8,6,5,8,128]{4,3,2,1,0:T(8,128)} %to_spatial.3), calls=%async_computation.1 | async-start | bytes 1966080 | tf_op jit(solution)/shard_map/all_to_all | solution.py:331
  118.8 4.7 %collective-permute-start.6 = (f32[6,4,48,128]{3,2,1,0:T(8,128)}, f32[6,4,48,128]{3,2,1,0:T(8,128)S(1)}, u32[]{:S(2)}, u32[]{:S(2)}) collective-permute-start(f32[6,4,48,128]{3,2,1,0:T(8,128)} %to_spectral.4.here), channel_id=1, source_target_pairs={{2,0},{0,2},{3,1},{1,3},{6,4},{4,6},{7,5},{5,7},{10,8},{8,10},{11,... | collective-permute-start | bytes 1769480 | tf_op jit(solution)/shard_map/ppermute | solution.py:273
  125.9 25.5 %collective-permute-done.6.other = f32[6,4,48,128]{3,2,1,0:T(8,128)S(1)} collective-permute-done((f32[6,4,48,128]{3,2,1,0:T(8,128)}, f32[6,4,48,128]{3,2,1,0:T(8,128)S(1)}, u32[]{:S(2)}, u32[]{:S(2)}) %collective-permute-start.6) | collective-permute-done | bytes 589856 | tf_op jit(solution)/shard_map/ppermute | solution.py:273
  152.2 2.9 %to_spatial.4 = f32[8,6,4,8,128]{4,3,2,1,0:T(8,128)} custom-call(f32[6,4,48,128]{3,2,1,0:T(8,128)} %to_spectral.4.here, f32[6,4,48,128]{3,2,1,0:T(8,128)} %copy-done.13, f32[6,6,48,128]{3,2,1,0:T(8,128)} %bitcast.44, bf16[64,48]{1,0:T(8,128)(2,1)} %get-tuple-element.44.first_hi, bf16[64,48]{1,0:T(8,128)(2,1)} %get-tuple-element.45.first_lo), custom_call_target="tpu_custom_call" | custom-call | flops 377487360 | bytes 1769472 | tf_op jit(solution)/shard_map/to_spatial/pallas_call | solution.py:223
  155.1 4.4 %all-to-all-start.4 = ((f32[8,6,4,8,128]{4,3,2,1,0:T(8,128)}), f32[8,6,4,8,128]{4,3,2,1,0:T(8,128)S(1)}, u32[]{:S(2)}, u32[]{:S(2)}) async-start(f32[8,6,4,8,128]{4,3,2,1,0:T(8,128)} %to_spatial.4), calls=%async_computation.4 | async-start | bytes 1572864 | tf_op jit(solution)/shard_map/all_to_all | solution.py:331
  159.5 4.4 %collective-permute-start.7 = (f32[6,4,48,128]{3,2,1,0:T(8,128)S(1)}, f32[6,4,48,128]{3,2,1,0:T(8,128)S(1)}, u32[]{:S(2)}, u32[]{:S(2)}) collective-permute-start(f32[6,4,48,128]{3,2,1,0:T(8,128)S(1)} %copy-done.2), channel_id=1, source_target_pairs={{2,0},{0,2},{3,1},{1,3},{6,4},{4,6},{7,5},{5,7},{10,8},{8,10},{11,... | collective-permute-start | bytes 1769480 | tf_op jit(solution)/shard_map/ppermute | solution.py:273
  163.9 8.3 %pairs_inverse.3 = (f32[2,8,128,128]{3,2,1,0:T(8,128)}, f32[2,8,128,128]{3,2,1,0:T(8,128)}, f32[2,8,128,128]{3,2,1,0:T(8,128)}, f32[2,8,128,128]{3,2,1,0:T(8,128)}) custom-call(s32[2]{0:T(128)} %add_convert_fusion.flags, f32[2,8,128,128]{3,2,1,0:T(8,128)} %collective-permute-done.refs_0_, f32[2,8,128,128]{3,2,1,0:T(8,128)} %collective-permute-done.4.refs_1_, ...), custom_call_target="tpu_custom_call" | custom-call | flops 5398069248 | bytes 12582912 | tf_op jit(solution)/shard_map/pairs_inverse/pallas_call | solution.py:172
  173.5 7.9 %pairs_inverse.4 = (f32[2,8,128,128]{3,2,1,0:T(8,128)}, f32[2,8,128,128]{3,2,1,0:T(8,128)}, f32[2,8,128,128]{3,2,1,0:T(8,128)}, f32[2,8,128,128]{3,2,1,0:T(8,128)}) custom-call(s32[2]{0:T(128)} %add_convert_fusion.flags, f32[2,8,128,128]{3,2,1,0:T(8,128)} %collective-permute-done.refs_0_, f32[2,8,128,128]{3,2,1,0:T(8,128)} %copy-done.15, ...), custom_call_target="tpu_custom_call" | custom-call | flops 4152360960 | bytes 12582912 | tf_op jit(solution)/shard_map/pairs_inverse/pallas_call | solution.py:172
  181.4 10.5 %collective-permute-done.7.other = f32[6,4,48,128]{3,2,1,0:T(8,128)S(1)} collective-permute-done((f32[6,4,48,128]{3,2,1,0:T(8,128)S(1)}, f32[6,4,48,128]{3,2,1,0:T(8,128)S(1)}, u32[]{:S(2)}, u32[]{:S(2)}) %collective-permute-start.7) | collective-permute-done | bytes 589856 | tf_op jit(solution)/shard_map/ppermute | solution.py:273
  192.8 2.9 %to_spatial.5 = f32[8,6,4,8,128]{4,3,2,1,0:T(8,128)} custom-call(f32[6,4,48,128]{3,2,1,0:T(8,128)} %to_spectral.5.here, f32[6,4,48,128]{3,2,1,0:T(8,128)} %copy-done.12, f32[6,6,48,128]{3,2,1,0:T(8,128)} %bitcast.45, bf16[64,48]{1,0:T(8,128)(2,1)} %get-tuple-element.44.first_hi, bf16[64,48]{1,0:T(8,128)(2,1)} %get-tuple-element.45.first_lo), custom_call_target="tpu_custom_call" | custom-call | flops 377487360 | bytes 1769472 | tf_op jit(solution)/shard_map/to_spatial/pallas_call | solution.py:223
  195.7 4.4 %all-to-all-start.5 = ((f32[8,6,4,8,128]{4,3,2,1,0:T(8,128)}), f32[8,6,4,8,128]{4,3,2,1,0:T(8,128)}, u32[]{:S(2)}, u32[]{:S(2)}) async-start(f32[8,6,4,8,128]{4,3,2,1,0:T(8,128)} %to_spatial.5), calls=%async_computation.5 | async-start | bytes 1572864 | tf_op jit(solution)/shard_map/all_to_all | solution.py:331
  200.1 3.3 %collective-permute-start.9 = (f32[2,8,128,128]{3,2,1,0:T(8,128)}, f32[2,8,128,128]{3,2,1,0:T(8,128)S(1)}, u32[]{:S(2)}, u32[]{:S(2)}) collective-permute-start(f32[2,8,128,128]{3,2,1,0:T(8,128)} %get-tuple-element.61), channel_id=1, source_target_pairs={{16,0},{32,16},{48,32},{0,48},{17,1},{33,17},{49,33},{1,49},{18,2}... | collective-permute-start | bytes 3145736 | tf_op jit(solution)/shard_map/ppermute | solution.py:273
  203.4 10.0 %all-to-all-done.5 = f32[8,6,4,8,128]{4,3,2,1,0:T(8,128)} async-done(((f32[8,6,4,8,128]{4,3,2,1,0:T(8,128)}), f32[8,6,4,8,128]{4,3,2,1,0:T(8,128)}, u32[]{:S(2)}, u32[]{:S(2)}) %all-to-all-start.5) | async-done | bytes 786464 | tf_op jit(solution)/shard_map/all_to_all | solution.py:331
  213.3 7.8 %pairs_inverse.5 = (f32[2,8,128,128]{3,2,1,0:T(8,128)}, f32[2,8,128,128]{3,2,1,0:T(8,128)}, f32[2,8,128,128]{3,2,1,0:T(8,128)}) custom-call(s32[2]{0:T(128)} %add_convert_fusion.flags, f32[2,8,128,128]{3,2,1,0:T(8,128)} %copy-done.15, f32[2,8,128,128]{3,2,1,0:T(8,128)} %broadcast_multiply_fusion.refs_2_.refs_1_, ...), custom_call_target="tpu_custom_call" | custom-call | flops 4152360960 | bytes 12582912 | tf_op jit(solution)/shard_map/pairs_inverse/pallas_call | solution.py:172
  222.9 3.0 %collective-permute-done.11 = f32[2,8,128,128]{3,2,1,0:T(8,128)S(1)} collective-permute-done((f32[2,8,128,128]{3,2,1,0:T(8,128)}, f32[2,8,128,128]{3,2,1,0:T(8,128)S(1)}, u32[]{:S(2)}, u32[]{:S(2)}) %collective-permute-start.11) | collective-permute-done | bytes 1048608 | tf_op jit(solution)/shard_map/ppermute | solution.py:273
  227.6 21.6 %collective-permute-done.9 = f32[2,8,128,128]{3,2,1,0:T(8,128)S(1)} collective-permute-done((f32[2,8,128,128]{3,2,1,0:T(8,128)}, f32[2,8,128,128]{3,2,1,0:T(8,128)S(1)}, u32[]{:S(2)}, u32[]{:S(2)}) %collective-permute-start.9) | collective-permute-done | bytes 1048608 | tf_op jit(solution)/shard_map/ppermute | solution.py:273
  249.2 3.3 %collective-permute-done.8 = f32[2,8,128,128]{3,2,1,0:T(8,128)S(1)} collective-permute-done((f32[2,8,128,128]{3,2,1,0:T(8,128)}, f32[2,8,128,128]{3,2,1,0:T(8,128)S(1)}, u32[]{:S(2)}, u32[]{:S(2)}) %collective-permute-start.8) | collective-permute-done | bytes 1048608 | tf_op jit(solution)/shard_map/ppermute | solution.py:273
  (74 shorter events, 27.6 us)
Async XLA Ops:
  3.2 25.5 %collective-permute-start = (f32[2,8,128,128]{3,2,1,0:T(8,128)}, f32[2,8,128,128]{3,2,1,0:T(8,128)}, u32[]{:S(2)}, u32[]{:S(2)}) collective-permute-start(f32[2,8,128,128]{3,2,1,0:T(8,128)} %broadcast_multiply_fusion.refs_2_.refs_1_), channel_id=1, source_target_pairs={{16,0},{32,16},{48,32},{0,48},{17,1},{33,17},{49,33},{1,49},{18,2}... | collective-permute-start | bytes 3145736 | tf_op jit(solution)/shard_map/ppermute | solution.py:273
  6.0 26.4 %collective-permute-start.2 = (f32[2,8,128,128]{3,2,1,0:T(8,128)}, f32[2,8,128,128]{3,2,1,0:T(8,128)}, u32[]{:S(2)}, u32[]{:S(2)}) collective-permute-start(f32[2,8,128,128]{3,2,1,0:T(8,128)} %broadcast_multiply_fusion.refs_2_.refs_1_), channel_id=1, source_target_pairs={{64,0},{128,64},{192,128},{0,192},{65,1},{129,65},{193,129},{1,193... | collective-permute-start | bytes 3145736 | tf_op jit(solution)/shard_map/ppermute | solution.py:273
  6.1 26.3 %collective-permute-start.4 = (f32[2,8,128,128]{3,2,1,0:T(8,128)}, f32[2,8,128,128]{3,2,1,0:T(8,128)}, u32[]{:S(2)}, u32[]{:S(2)}) collective-permute-start(f32[2,8,128,128]{3,2,1,0:T(8,128)} %broadcast_multiply_fusion.refs_2_.refs_1_), channel_id=1, source_target_pairs={{48,0},{0,16},{16,32},{32,48},{49,1},{1,17},{17,33},{33,49},{50,2}... | collective-permute-start | bytes 3145736 | tf_op jit(solution)/shard_map/ppermute | solution.py:273
  6.1 4.2 %copy-start.14 = (s32[128]{0:T(128)}, s32[128]{0:T(128)S(1)}, u32[]{:S(2)}) copy-start(s32[128]{0:T(128)S(1)} %iota_add_fusion.1) | copy-start | bytes 1540
  11.6 3.4 %copy-start.4 = (f32[1,256,256]{2,1,0:T(8,128)S(1)}, f32[1,256,256]{2,1,0:T(8,128)}, u32[]{:S(2)}) copy-start(f32[1,256,256]{2,1,0:T(8,128)} %get-tuple-element.69) | copy-start | bytes 786436
  11.6 3.4 %copy-start.5 = (f32[1,256,256]{2,1,0:T(8,128)S(1)}, f32[1,256,256]{2,1,0:T(8,128)}, u32[]{:S(2)}) copy-start(f32[1,256,256]{2,1,0:T(8,128)} %get-tuple-element.70) | copy-start | bytes 786436
  11.7 3.4 %copy-start.6 = (f32[1,256,256]{2,1,0:T(8,128)S(1)}, f32[1,256,256]{2,1,0:T(8,128)}, u32[]{:S(2)}) copy-start(f32[1,256,256]{2,1,0:T(8,128)} %get-tuple-element.71) | copy-start | bytes 786436
  11.7 3.4 %copy-start.7 = (f32[1,256,256]{2,1,0:T(8,128)S(1)}, f32[1,256,256]{2,1,0:T(8,128)}, u32[]{:S(2)}) copy-start(f32[1,256,256]{2,1,0:T(8,128)} %get-tuple-element.72) | copy-start | bytes 786436
  28.7 25.6 %collective-permute-start.1 = (f32[2,8,128,128]{3,2,1,0:T(8,128)}, f32[2,8,128,128]{3,2,1,0:T(8,128)S(1)}, u32[]{:S(2)}, u32[]{:S(2)}) collective-permute-start(f32[2,8,128,128]{3,2,1,0:T(8,128)} %collective-permute-done.refs_0_), channel_id=1, source_target_pairs={{16,0},{32,16},{48,32},{0,48},{17,1},{33,17},{49,33},{1,49},{18,2}... | collective-permute-start | bytes 3145736 | tf_op jit(solution)/shard_map/ppermute | solution.py:273
  39.5 22.2 %all-to-all-start = ((f32[8,6,5,8,128]{4,3,2,1,0:T(8,128)}), f32[8,6,5,8,128]{4,3,2,1,0:T(8,128)S(1)}, u32[]{:S(2)}, u32[]{:S(2)}) async-start(f32[8,6,5,8,128]{4,3,2,1,0:T(8,128)} %bitcast.47), calls=%async_computation | async-start | bytes 1966080 | tf_op jit(solution)/shard_map/all_to_all | solution.py:331
  43.9 30.3 %collective-permute-start.3 = (f32[2,8,128,128]{3,2,1,0:T(8,128)}, f32[2,8,128,128]{3,2,1,0:T(8,128)}, u32[]{:S(2)}, u32[]{:S(2)}) collective-permute-start(f32[2,8,128,128]{3,2,1,0:T(8,128)} %collective-permute-done.2.refs_3_.refs_2_), channel_id=1, source_target_pairs={{64,0},{128,64},{192,128},{0,192},{65,1},{129,65},{193,129},{1,193... | collective-permute-start | bytes 3145736 | tf_op jit(solution)/shard_map/ppermute | solution.py:273
  54.3 1.0 copy-start.15
  61.6 4.5 %copy-start.9 = (f32[8,6,5,8,128]{4,3,2,1,0:T(8,128)}, f32[8,6,5,8,128]{4,3,2,1,0:T(8,128)S(1)}, u32[]{:S(2)}) copy-start(f32[8,6,5,8,128]{4,3,2,1,0:T(8,128)S(1)} %all-to-all-done.given) | copy-start | bytes 2949124
  61.6 19.2 %all-to-all-start.3 = ((f32[8,6,4,8,128]{4,3,2,1,0:T(8,128)}), f32[8,6,4,8,128]{4,3,2,1,0:T(8,128)S(1)}, u32[]{:S(2)}, u32[]{:S(2)}) async-start(f32[8,6,4,8,128]{4,3,2,1,0:T(8,128)} %bitcast.49), calls=%async_computation.3 | async-start | bytes 1572864 | tf_op jit(solution)/shard_map/all_to_all | solution.py:331
  68.8 39.3 %collective-permute-start.5 = (f32[6,5,48,128]{3,2,1,0:T(8,128)}, f32[6,5,48,128]{3,2,1,0:T(8,128)S(1)}, u32[]{:S(2)}, u32[]{:S(2)}) collective-permute-start(f32[6,5,48,128]{3,2,1,0:T(8,128)} %to_spectral.3.here), channel_id=1, source_target_pairs={{2,0},{0,2},{3,1},{1,3},{6,4},{4,6},{7,5},{5,7},{10,8},{8,10},{11,... | collective-permute-start | bytes 2211848 | tf_op jit(solution)/shard_map/ppermute | solution.py:273
  80.8 31.2 %copy-start = (f32[8,6,4,8,128]{4,3,2,1,0:T(8,128)}, f32[8,6,4,8,128]{4,3,2,1,0:T(8,128)S(1)}, u32[]{:S(2)}) copy-start(f32[8,6,4,8,128]{4,3,2,1,0:T(8,128)S(1)} %all-to-all-done.3.given) | copy-start | bytes 2359300
  80.9 31.2 %all-to-all-start.2 = ((f32[8,6,4,8,128]{4,3,2,1,0:T(8,128)}), f32[8,6,4,8,128]{4,3,2,1,0:T(8,128)S(1)}, u32[]{:S(2)}, u32[]{:S(2)}) async-start(f32[8,6,4,8,128]{4,3,2,1,0:T(8,128)} %bitcast.50), calls=%async_computation.2 | async-start | bytes 1572864 | tf_op jit(solution)/shard_map/all_to_all | solution.py:331
  112.1 4.4 %copy-start.1 = (f32[8,6,4,8,128]{4,3,2,1,0:T(8,128)}, f32[8,6,4,8,128]{4,3,2,1,0:T(8,128)S(1)}, u32[]{:S(2)}) copy-start(f32[8,6,4,8,128]{4,3,2,1,0:T(8,128)S(1)} %all-to-all-done.2.given) | copy-start | bytes 2359300
  112.1 43.0 %all-to-all-start.1 = ((f32[8,6,5,8,128]{4,3,2,1,0:T(8,128)}), f32[8,6,5,8,128]{4,3,2,1,0:T(8,128)S(1)}, u32[]{:S(2)}, u32[]{:S(2)}) async-start(f32[8,6,5,8,128]{4,3,2,1,0:T(8,128)} %to_spatial.3), calls=%async_computation.1 | async-start | bytes 1966080 | tf_op jit(solution)/shard_map/all_to_all | solution.py:331
  118.8 32.5 %collective-permute-start.6 = (f32[6,4,48,128]{3,2,1,0:T(8,128)}, f32[6,4,48,128]{3,2,1,0:T(8,128)S(1)}, u32[]{:S(2)}, u32[]{:S(2)}) collective-permute-start(f32[6,4,48,128]{3,2,1,0:T(8,128)} %to_spectral.4.here), channel_id=1, source_target_pairs={{2,0},{0,2},{3,1},{1,3},{6,4},{4,6},{7,5},{5,7},{10,8},{8,10},{11,... | collective-permute-start | bytes 1769480 | tf_op jit(solution)/shard_map/ppermute | solution.py:273
  125.9 33.6 %copy-start.2 = (f32[6,4,48,128]{3,2,1,0:T(8,128)S(1)}, f32[6,4,48,128]{3,2,1,0:T(8,128)}, u32[]{:S(2)}) copy-start(f32[6,4,48,128]{3,2,1,0:T(8,128)} %to_spectral.5.here) | copy-start | bytes 1769476
  155.1 8.9 %copy-start.8 = (f32[8,6,5,8,128]{4,3,2,1,0:T(8,128)}, f32[8,6,5,8,128]{4,3,2,1,0:T(8,128)S(1)}, u32[]{:S(2)}) copy-start(f32[8,6,5,8,128]{4,3,2,1,0:T(8,128)S(1)} %all-to-all-done.1) | copy-start | bytes 2949124
  155.1 17.5 %all-to-all-start.4 = ((f32[8,6,4,8,128]{4,3,2,1,0:T(8,128)}), f32[8,6,4,8,128]{4,3,2,1,0:T(8,128)S(1)}, u32[]{:S(2)}, u32[]{:S(2)}) async-start(f32[8,6,4,8,128]{4,3,2,1,0:T(8,128)} %to_spatial.4), calls=%async_computation.4 | async-start | bytes 1572864 | tf_op jit(solution)/shard_map/all_to_all | solution.py:331
  159.5 32.5 %collective-permute-start.7 = (f32[6,4,48,128]{3,2,1,0:T(8,128)S(1)}, f32[6,4,48,128]{3,2,1,0:T(8,128)S(1)}, u32[]{:S(2)}, u32[]{:S(2)}) collective-permute-start(f32[6,4,48,128]{3,2,1,0:T(8,128)S(1)} %copy-done.2), channel_id=1, source_target_pairs={{2,0},{0,2},{3,1},{1,3},{6,4},{4,6},{7,5},{5,7},{10,8},{8,10},{11,... | collective-permute-start | bytes 1769480 | tf_op jit(solution)/shard_map/ppermute | solution.py:273
  172.6 0.9 copy-start.10
  195.7 17.6 %all-to-all-start.5 = ((f32[8,6,4,8,128]{4,3,2,1,0:T(8,128)}), f32[8,6,4,8,128]{4,3,2,1,0:T(8,128)}, u32[]{:S(2)}, u32[]{:S(2)}) async-start(f32[8,6,4,8,128]{4,3,2,1,0:T(8,128)} %to_spatial.5), calls=%async_computation.5 | async-start | bytes 1572864 | tf_op jit(solution)/shard_map/all_to_all | solution.py:331
  200.1 25.8 %collective-permute-start.11 = (f32[2,8,128,128]{3,2,1,0:T(8,128)}, f32[2,8,128,128]{3,2,1,0:T(8,128)S(1)}, u32[]{:S(2)}, u32[]{:S(2)}) collective-permute-start(f32[2,8,128,128]{3,2,1,0:T(8,128)} %get-tuple-element.64), channel_id=1, source_target_pairs={{192,0},{0,64},{64,128},{128,192},{193,1},{1,65},{65,129},{129,193... | collective-permute-start | bytes 3145736 | tf_op jit(solution)/shard_map/ppermute | solution.py:273
  200.1 49.1 %collective-permute-start.9 = (f32[2,8,128,128]{3,2,1,0:T(8,128)}, f32[2,8,128,128]{3,2,1,0:T(8,128)S(1)}, u32[]{:S(2)}, u32[]{:S(2)}) collective-permute-start(f32[2,8,128,128]{3,2,1,0:T(8,128)} %get-tuple-element.61), channel_id=1, source_target_pairs={{16,0},{32,16},{48,32},{0,48},{17,1},{33,17},{49,33},{1,49},{18,2}... | collective-permute-start | bytes 3145736 | tf_op jit(solution)/shard_map/ppermute | solution.py:273
  203.4 49.1 %collective-permute-start.8 = (f32[2,8,128,128]{3,2,1,0:T(8,128)}, f32[2,8,128,128]{3,2,1,0:T(8,128)S(1)}, u32[]{:S(2)}, u32[]{:S(2)}) collective-permute-start(f32[2,8,128,128]{3,2,1,0:T(8,128)} %get-tuple-element.60), channel_id=1, source_target_pairs={{48,0},{0,16},{16,32},{32,48},{49,1},{1,17},{17,33},{33,49},{50,2}... | collective-permute-start | bytes 3145736 | tf_op jit(solution)/shard_map/ppermute | solution.py:273
  221.1 31.4 %copy-start.3 = (f32[2,8,128,128]{3,2,1,0:T(8,128)S(1)}, f32[2,8,128,128]{3,2,1,0:T(8,128)}, u32[]{:S(2)}) copy-start(f32[2,8,128,128]{3,2,1,0:T(8,128)} %get-tuple-element.59) | copy-start | bytes 3145732
  221.1 31.4 %collective-permute-start.10 = (f32[2,8,128,128]{3,2,1,0:T(8,128)}, f32[2,8,128,128]{3,2,1,0:T(8,128)S(1)}, u32[]{:S(2)}, u32[]{:S(2)}) collective-permute-start(f32[2,8,128,128]{3,2,1,0:T(8,128)} %get-tuple-element.62), channel_id=1, source_target_pairs={{32,0},{48,16},{0,32},{16,48},{33,1},{49,17},{1,33},{17,49},{34,2}... | collective-permute-start | bytes 3145736 | tf_op jit(solution)/shard_map/ppermute | solution.py:273
  227.2 25.3 %collective-permute-start.12 = (f32[2,8,128,128]{3,2,1,0:T(8,128)S(1)}, f32[2,8,128,128]{3,2,1,0:T(8,128)S(1)}, u32[]{:S(2)}, u32[]{:S(2)}) collective-permute-start(f32[2,8,128,128]{3,2,1,0:T(8,128)S(1)} %add.286), channel_id=1, source_target_pairs={{192,0},{0,64},{64,128},{128,192},{193,1},{1,65},{65,129},{129,193... | collective-permute-start | bytes 3145736 | tf_op jit(solution)/shard_map/ppermute | solution.py:273
  (3 other events, 2.5 us)
